TPU v7x, 32 devices: a whole 2x2x4 slice. The times are simulated.
32 devices in a mesh: slab: 2 (over x), shot: 8 (over z, y), rcv: 2 (over core).
Axes of the slice: x: 2, y: 2, z: 4, core: 2. Of those that a mesh axis runs over, the one named last changes fastest.
Arguments:
- traces: bfloat16 [16, 256, 1536], P(('slab', 'shot'), 'rcv'), parts along dimension 0, may hold values from -6 to 6
- rcv_delay: int32 [16, 256, 9], P(('slab', 'shot'), 'rcv'), parts along dimension 0, may hold values from 0 to 47
- rcv_frac: int32 [16, 256, 9], P(('slab', 'shot'), 'rcv'), parts along dimension 0, may hold values from 0 to 255
- live_count: int32 [16], P(('slab', 'shot')), parts along dimension 0, may hold values from 64 to 256
- src_delay: int32 [16, 2, 128, 9], P('slab', 'rcv', 'shot'), parts along dimension 0, may hold values from 0 to 47
- src_frac: int32 [16, 2, 128, 9], P('slab', 'rcv', 'shot'), parts along dimension 0, may hold values from 0 to 255
- rcv_taper: float32 [9], replicated, may hold values from 0.5 to 1.5
- src_taper: float32 [9], replicated, may hold values from 0.5 to 1.5
Outputs:
- redatumed: bfloat16 [16, 2, 128, 1536], P('slab', 'rcv', 'shot'), parts along dimension 0
There are 2 independent parts, one for each index of `slab`. A program takes and returns all parts, laid end to end along the dimension named above; an argument that names none is the same for every part. Nothing has to cross between parts.
All inputs are finite; a program needn't handle non-finite values.
Results may differ from a plain program's by a relative error of at most 0.0055.
Values may be sent and summed in bfloat16 or wider, within the bound.
A program may use at most 64 MiB of HBM per device.

v0:
```python
import functools

import jax
import jax.numpy as jnp
import numpy as np
from jax import lax
from jax.experimental import pallas as pl
from jax.experimental.pallas import tpu as pltpu
from jax.sharding import PartitionSpec as P

AR = 4
AS = 4
TRI = 2
LANES = 128
GROUP = 8
EDGE = 16
MESH = pl.DeviceIdType.MESH


def taps_of_filter():
    heights = np.maximum(TRI - np.abs(np.arange(-TRI, TRI + 1)), 0).astype(np.float32)
    taps = (heights / np.sqrt(np.sum(heights**2, dtype=np.float32))).astype(jnp.bfloat16)
    return [float(v) for v in taps[TRI:]]


MAIN_TAP, SIDE_TAP = taps_of_filter()[:2]


def ends(shape):
    lane = lax.broadcasted_iota(jnp.int32, shape, 1)
    return lane == 0, lane == LANES - 1


def smooth(raw):
    is_first, is_last = ends(raw[0].shape)
    zero = jnp.zeros_like(raw[0])
    up = [zero] + [pltpu.roll(x, 1, 1) for x in raw]
    down = [pltpu.roll(x, LANES - 1, 1) for x in raw] + [zero]
    done = []
    for b, x in enumerate(raw):
        before = jnp.where(is_first, up[b], up[b + 1])
        after = jnp.where(is_last, down[b + 1], down[b])
        done.append((MAIN_TAP * x + SIDE_TAP * (before + after)).astype(jnp.bfloat16))
    return done


def ahead(values):
    _, is_last = ends(values[0].shape)
    rolled = [pltpu.roll(x, LANES - 1, 1) for x in values] + [jnp.zeros_like(values[0])]
    return [jnp.where(is_last, rolled[b + 1], rolled[b]) for b in range(len(values))]


def gathered(idx, own, mixed, nb):
    now = mixed(0)
    for b in range(nb):
        after = mixed(b + 1) if b + 1 < nb else jnp.zeros_like(now)
        yield b, jnp.take_along_axis(jnp.where(own, now, after), idx, axis=1)
        now = after


def kernel(
    dims,
    live_hbm, rtaper_hbm, staper_hbm, x_hbm, rd_hbm, rf_hbm, sd_hbm, sf_hbm,
    out_ref,
    live_ref, rtaper_ref, staper_ref, x_ref, rd_ref, rf_ref, sd_ref, sf_ref, in_sem,
    flat, turned, near, near1, far, far1, halo, sec, got, acc,
    r_d, r_c0, r_c1, r_norm, t_d, t_c0, t_c1,
    halo_send, halo_recv, send_sem, recv_sem,
):
    rows, nt, peers, per_peer, n_rcv, kr, ks = dims
    nb = nt // LANES
    chunks = pl.cdiv(per_peer, GROUP)
    used = min(GROUP, per_peer)
    me = lax.axis_index("shot")
    side = lax.axis_index("rcv")
    other = 1 - side
    f32 = jnp.float32

    pairs = (
        (rd_hbm, rd_ref), (rf_hbm, rf_ref), (x_hbm.at[0], x_ref), (live_hbm, live_ref),
        (rtaper_hbm, rtaper_ref), (staper_hbm, staper_ref), (sd_hbm, sd_ref), (sf_hbm, sf_ref),
    )
    loads = [pltpu.make_async_copy(a, b, in_sem.at[n]) for n, (a, b) in enumerate(pairs)]
    for load in loads:
        load.start()

    barrier = pltpu.get_barrier_semaphore()

    def greet(i, carry):
        to = lax.rem(me + i, peers)
        pl.semaphore_signal(barrier, inc=1, device_id={"shot": to}, device_id_type=MESH)
        return carry

    pl.semaphore_signal(barrier, inc=1, device_id={"rcv": other}, device_id_type=MESH)
    lax.fori_loop(1, peers, greet, 0)

    for b in range(nb):
        for start in (0, EDGE + rows):
            near[b, start : start + EDGE, :] = jnp.zeros((EDGE, LANES), f32)
            near1[b, start : start + EDGE, :] = jnp.zeros((EDGE, LANES), f32)
    flat[...] = jnp.zeros_like(flat)

    lane = lax.broadcasted_iota(jnp.int32, (GROUP, LANES), 1)
    sub = lax.broadcasted_iota(jnp.int32, (GROUP, LANES), 0)

    def spread(column):
        packed = jnp.broadcast_to(column, (GROUP, LANES))
        return packed >> 8, (packed & 255).astype(f32) * (1.0 / 256.0)

    loads[0].wait()
    loads[1].wait()
    loads[3].wait()
    loads[4].wait()
    live_count = live_ref[0]
    for block in range(rows // LANES):
        cols = slice(block * LANES, (block + 1) * LANES)
        for a in range(kr):
            flat[a : a + 1, :] = rd_ref[a, :, cols] * 256 + rf_ref[a, :, cols]
        turned[block] = jnp.transpose(flat[...], (1, 0))

    def receiver_tables(g, carry):
        at = pl.ds(pl.multiple_of(g * GROUP, GROUP), GROUP)
        columns = turned[g // (LANES // GROUP), pl.ds(pl.multiple_of(lax.rem(g, LANES // GROUP) * GROUP, GROUP), GROUP), :]
        where0 = side * rows + g * GROUP + sub - AR
        fold = jnp.zeros((GROUP, LANES), f32)
        for a in range(kr):
            d, weight = spread(columns[:, a : a + 1])
            where = where0 + a
            live = (where >= 0) & (where < rows * n_rcv) & (where < live_count)
            live = live.astype(f32)
            fold = fold + live
            scale = rtaper_ref[a] * live
            r_d[a, at, :] = d
            r_c0[a, at, :] = scale * (1.0 - weight)
            r_c1[a, at, :] = scale * weight
        r_norm[at, :] = 1.0 / jnp.sqrt(jnp.maximum(fold, 1.0))
        return carry

    lax.fori_loop(0, rows // GROUP, receiver_tables, 0)

    pl.semaphore_wait(barrier, peers)

    halo_copy = pltpu.make_async_remote_copy(
        src_ref=x_hbm.at[0, pl.ds(pl.multiple_of(other * (rows - EDGE), EDGE), EDGE), :],
        dst_ref=halo,
        send_sem=halo_send,
        recv_sem=halo_recv,
        device_id={"rcv": other},
        device_id_type=MESH,
    )
    halo_copy.start()

    def filter_rows(load, base):
        done = [v.astype(f32) for v in smooth([load(b).astype(f32) for b in range(nb)])]
        for b, (value, value1) in enumerate(zip(done, ahead(done))):
            near[b, pl.ds(base, EDGE), :] = value
            near1[b, pl.ds(base, EDGE), :] = value1

    def filter_own(g, carry):
        start = pl.multiple_of(g * EDGE, EDGE)
        filter_rows(lambda b: x_ref[pl.ds(start, EDGE), b * LANES : (b + 1) * LANES], EDGE + start)
        return carry

    loads[2].wait()
    lax.fori_loop(0, rows // EDGE, filter_own, 0)

    edge_peer = other * (peers - 1)

    def partner(i, sign):
        step = peers // 2 + (1 - 2 * lax.rem(i, 2)) * ((i + 1) // 2)
        return lax.rem(me + sign * step + 2 * peers, peers)

    def send_of(to):
        return pltpu.make_async_remote_copy(
            src_ref=sec.at[to],
            dst_ref=got.at[me],
            send_sem=send_sem.at[to],
            recv_sem=recv_sem.at[me],
            device_id={"shot": to},
            device_id_type=MESH,
        )

    def recv_of(origin):
        return pltpu.make_async_remote_copy(
            src_ref=sec.at[origin],
            dst_ref=got.at[origin],
            send_sem=send_sem.at[origin],
            recv_sem=recv_sem.at[origin],
            device_id={"shot": origin},
            device_id_type=MESH,
        )

    def receiver_step(i, carry):
        to = partner(i, 1)

        @pl.when(to == edge_peer)
        def _():
            halo_copy.wait_recv()
            filter_rows(
                lambda b: halo[:, b * LANES : (b + 1) * LANES],
                pl.multiple_of(other * (EDGE + rows), EDGE),
            )

        for c in range(chunks):
            row0 = to * per_peer + c * GROUP
            if per_peer % GROUP == 0:
                row0 = pl.multiple_of(row0, GROUP)
            at = pl.ds(row0, GROUP)
            total = [None] * nb
            for a in range(kr):
                d, c0, c1 = r_d[a, at, :], r_c0[a, at, :], r_c1[a, at, :]
                source = pl.ds(EDGE - AR + row0 + a, GROUP)

                def mixed(b):
                    return c0 * near[b, source, :] + c1 * near1[b, source, :]

                for b, value in gathered((lane + d) & (LANES - 1), lane >= d, mixed, nb):
                    total[b] = value if a == 0 else total[b] + value
            norm = r_norm[at, :]
            one = [(v * norm).astype(jnp.bfloat16).astype(f32) for v in total]
            for b, value in enumerate(smooth(one)):
                sec[to, c * GROUP : c * GROUP + used, b * LANES : (b + 1) * LANES] = value[:used]

        @pl.when(i < peers - 1)
        def _():
            send_of(to).start()

        return carry

    lax.fori_loop(0, peers, receiver_step, 0)

    for n in (5, 6, 7):
        loads[n].wait()
    group = LANES // EDGE

    def source_tables(g, carry):
        for kk in range(group):
            for a in range(ks):
                at = kk * EDGE + a
                flat[at : at + 1, :per_peer] = sd_ref[g * group + kk, a] * 256 + sf_ref[g * group + kk, a]
        turned[0] = jnp.transpose(flat[...], (1, 0))
        for kk in range(group):
            k = g * group + kk
            count = jnp.minimum(k + ks - AS, peers) - jnp.maximum(k - AS, 0)
            norm = 1.0 / jnp.sqrt(jnp.full((GROUP, LANES), count, jnp.int32).astype(f32))
            for c in range(chunks):
                at = slice(c * GROUP, c * GROUP + GROUP)
                columns = turned[0, at, :]
                for a in range(ks):
                    d, weight = spread(columns[:, kk * EDGE + a : kk * EDGE + a + 1])
                    scale = staper_ref[a] * norm
                    t_d[k, a, at, :] = d
                    t_c0[k, a, at, :] = scale * (1.0 - weight)
                    t_c1[k, a, at, :] = scale * weight
        return carry

    lax.fori_loop(0, peers // group, source_tables, 0)

    def clear(k, carry):
        for b in range(nb):
            acc[k, b] = jnp.zeros(acc.shape[2:], f32)
        return carry

    lax.fori_loop(0, peers, clear, 0)

    if per_peer < GROUP:
        for b in range(nb):
            far[b] = jnp.zeros(far.shape[1:], f32)
            far1[b] = jnp.zeros(far.shape[1:], f32)
    width = min(peers, ks)

    def shot_sum(p, block_of):
        done = [block_of(b).astype(f32) for b in range(nb)]
        for b, (value, value1) in enumerate(zip(done, ahead(done))):
            far[b, :per_peer, :] = value
            far1[b, :per_peer, :] = value1
        base = 0 if width == peers else jnp.minimum(jnp.maximum(p - AS, 0), peers - width)
        for kk in range(width):
            k = base + kk
            tap = p - k + AS
            a = jnp.minimum(jnp.maximum(tap, 0), ks - 1)
            inside = jnp.where(tap == a, 1.0, 0.0)
            for c in range(chunks):
                at = slice(c * GROUP, c * GROUP + GROUP)
                d, c0, c1 = t_d[k, a, at, :], t_c0[k, a, at, :] * inside, t_c1[k, a, at, :] * inside

                def mixed(b):
                    return c0 * far[b, at, :] + c1 * far1[b, at, :]

                for b, value in gathered((lane + d) & (LANES - 1), lane >= d, mixed, nb):
                    acc[k, b, at, :] += value

    shot_sum(me, lambda b: sec[me, :, b * LANES : (b + 1) * LANES])

    def source_step(i, carry):
        origin = partner(i, -1)
        recv_of(origin).wait_recv()
        shot_sum(origin, lambda b: got[origin, :, b * LANES : (b + 1) * LANES])
        return carry

    lax.fori_loop(0, peers - 1, source_step, 0)

    def finish(k, carry):
        for b in range(nb):
            out_ref[k, 0, :, b * LANES : (b + 1) * LANES] = acc[k, b, :per_peer, :].astype(jnp.bfloat16)
        return carry

    lax.fori_loop(0, peers, finish, 0)

    halo_copy.wait_send()

    def drain(i, carry):
        send_of(partner(i, 1)).wait_send()
        return carry

    lax.fori_loop(0, peers - 1, drain, 0)


def body(traces, rcv_delay, rcv_frac, live_count, src_delay, src_frac, rcv_taper, src_taper):
    _, rows, nt = traces.shape
    peers = lax.axis_size("shot")
    n_rcv = lax.axis_size("rcv")
    per_peer = rows // peers
    kr, ks = rcv_delay.shape[-1], src_delay.shape[-1]
    nb = nt // LANES
    tall = pl.cdiv(per_peer, GROUP) * GROUP
    rcv_delay, rcv_frac = (jnp.transpose(v, (2, 0, 1)) for v in (rcv_delay, rcv_frac))
    src_delay, src_frac = (jnp.transpose(v, (0, 3, 1, 2)) for v in (src_delay, src_frac))
    dims = (rows, nt, peers, per_peer, n_rcv, kr, ks)
    hbm = pl.BlockSpec(memory_space=pltpu.HBM)
    f32, bf16, i32 = jnp.float32, jnp.bfloat16, jnp.int32
    extended = (nb, rows + 2 * EDGE, LANES)
    r_table = (kr, rows + GROUP, LANES)
    t_table = (peers, ks, tall, LANES)
    return pl.pallas_call(
        functools.partial(kernel, dims),
        name="redatum",
        out_shape=jax.ShapeDtypeStruct((peers, 1, per_peer, nt), bf16),
        in_specs=[hbm] * 8,
        out_specs=pl.BlockSpec(memory_space=pltpu.VMEM),
        scratch_shapes=[
            pltpu.SMEM((1,), i32),
            pltpu.SMEM((kr,), f32),
            pltpu.SMEM((ks,), f32),
            pltpu.VMEM((rows, nt), bf16),
            pltpu.VMEM(rcv_delay.shape, i32),
            pltpu.VMEM(rcv_delay.shape, i32),
            pltpu.VMEM(src_delay.shape, i32),
            pltpu.VMEM(src_delay.shape, i32),
            pltpu.SemaphoreType.DMA((8,)),
            pltpu.VMEM((LANES, LANES), i32),
            pltpu.VMEM((rows // LANES, LANES, LANES), i32),
            pltpu.VMEM(extended, f32),
            pltpu.VMEM(extended, f32),
            pltpu.VMEM((nb, tall, LANES), f32),
            pltpu.VMEM((nb, tall, LANES), f32),
            pltpu.VMEM((EDGE, nt), bf16),
            pltpu.VMEM((peers, per_peer, nt), bf16),
            pltpu.VMEM((peers, per_peer, nt), bf16),
            pltpu.VMEM((peers, nb, tall, LANES), f32),
            pltpu.VMEM(r_table, i32),
            pltpu.VMEM(r_table, f32),
            pltpu.VMEM(r_table, f32),
            pltpu.VMEM(r_table[1:], f32),
            pltpu.VMEM(t_table, i32),
            pltpu.VMEM(t_table, f32),
            pltpu.VMEM(t_table, f32),
            pltpu.SemaphoreType.DMA,
            pltpu.SemaphoreType.DMA,
            pltpu.SemaphoreType.DMA((peers,)),
            pltpu.SemaphoreType.DMA((peers,)),
        ],
        compiler_params=pltpu.CompilerParams(
            collective_id=0, has_side_effects=True, vmem_limit_bytes=67_043_328
        ),
    )(live_count, rcv_taper, src_taper, traces, rcv_delay, rcv_frac, src_delay, src_frac)


def solution(mesh):
    return jax.shard_map(
        body,
        mesh=mesh,
        in_specs=(
            P(("slab", "shot"), "rcv", None),
            P(("slab", "shot"), "rcv", None),
            P(("slab", "shot"), "rcv", None),
            P(("slab", "shot")),
            P("slab", "rcv", "shot", None),
            P("slab", "rcv", "shot", None),
            P(),
            P(),
        ),
        out_specs=P("slab", "rcv", "shot", None),
        check_vma=False,
    )
```

profile of v0, /device:TPU:0, one launch (start us, length us, event | category | flops | bytes accessed | tf_op | source)
XLA Modules:
  0.0 22.8 jit_solution(15631285374826298678)
XLA Ops:
  0.7 20.4 %redatum.1 = bf16[8,1,16,1536]{3,2,1,0:T(8,128)(2,1)} custom-call(s32[1]{0:T(128)S(6)} %copy.10.live_hbm, f32[9]{0:T(128)} %rtaper_hbm.1, f32[9]{0:T(128)} %staper_hbm.1, bf16[1,128,1536]{2,1,0:T(8,128)(2,1)} %x_hbm.1, s32[9,1,128]{2,1,0:T(1,128)} %bitcast.6, s32[9,1,128]{2,1,0:T(1,128)} %bitcast.7, s32[8,9,1,16]{3,2,1,0:T(1,128)} %bitcast.4, ...), custom_call_target="tpu_custom_call" | custom-call | tf_op jit(solution)/shard_map/redatum/pallas_call | solution.py:335
  21.0 1.8 %copy.11 = bf16[8,1,16,1536]{3,2,1,0:T(8,128)(2,1)} copy(bf16[8,1,16,1536]{3,2,1,0:T(8,128)(2,1)} %redatum.1) | data formatting | bytes 786432
where the time goes:
time: 23 us; the launch traced here: 22.8 us
  Pallas kernels  20.4 us (89%)
  local copies, waits for them, and re-layouts  1.77 us (8%)
  between operations  0.66 us (3%)
    pallas_call x1, Pallas kernels, body(): pl.pallas_call(functools.partial(kernel, dims), name='redatum', out_shape...  20.4 us
    unnamed x1, local copies, waits for them, and re-layouts  1.77 us

commit v1 on v0

--- a/solution.py
+++ b/solution.py
@@ -60,9 +60,9 @@
 
 def kernel(
     dims,
-    live_hbm, rtaper_hbm, staper_hbm, x_hbm, rd_hbm, rf_hbm, sd_hbm, sf_hbm,
+    live_hbm, rtaper_hbm, staper_hbm, x_hbm, rd_ref, rf_ref, sd_hbm, sf_hbm,
     out_ref,
-    live_ref, rtaper_ref, staper_ref, x_ref, rd_ref, rf_ref, sd_ref, sf_ref, in_sem,
+    live_ref, rtaper_ref, staper_ref, x_ref, sd_ref, sf_ref, in_sem,
     flat, turned, near, near1, far, far1, halo, sec, got, acc,
     r_d, r_c0, r_c1, r_norm, t_d, t_c0, t_c1,
     halo_send, halo_recv, send_sem, recv_sem,
@@ -77,8 +77,8 @@
     f32 = jnp.float32
 
     pairs = (
-        (rd_hbm, rd_ref), (rf_hbm, rf_ref), (x_hbm.at[0], x_ref), (live_hbm, live_ref),
-        (rtaper_hbm, rtaper_ref), (staper_hbm, staper_ref), (sd_hbm, sd_ref), (sf_hbm, sf_ref),
+        (x_hbm.at[0], x_ref), (live_hbm, live_ref), (rtaper_hbm, rtaper_ref),
+        (staper_hbm, staper_ref), (sd_hbm, sd_ref), (sf_hbm, sf_ref),
     )
     loads = [pltpu.make_async_copy(a, b, in_sem.at[n]) for n, (a, b) in enumerate(pairs)]
     for load in loads:
@@ -107,10 +107,8 @@
         packed = jnp.broadcast_to(column, (GROUP, LANES))
         return packed >> 8, (packed & 255).astype(f32) * (1.0 / 256.0)
 
-    loads[0].wait()
     loads[1].wait()
-    loads[3].wait()
-    loads[4].wait()
+    loads[2].wait()
     live_count = live_ref[0]
     for block in range(rows // LANES):
         cols = slice(block * LANES, (block + 1) * LANES)
@@ -161,7 +159,7 @@
         filter_rows(lambda b: x_ref[pl.ds(start, EDGE), b * LANES : (b + 1) * LANES], EDGE + start)
         return carry
 
-    loads[2].wait()
+    loads[0].wait()
     lax.fori_loop(0, rows // EDGE, filter_own, 0)
 
     edge_peer = other * (peers - 1)
@@ -229,7 +227,7 @@
 
     lax.fori_loop(0, peers, receiver_step, 0)
 
-    for n in (5, 6, 7):
+    for n in (3, 4, 5):
         loads[n].wait()
     group = LANES // EDGE
 
@@ -327,7 +325,9 @@
     rcv_delay, rcv_frac = (jnp.transpose(v, (2, 0, 1)) for v in (rcv_delay, rcv_frac))
     src_delay, src_frac = (jnp.transpose(v, (0, 3, 1, 2)) for v in (src_delay, src_frac))
     dims = (rows, nt, peers, per_peer, n_rcv, kr, ks)
-    hbm = pl.BlockSpec(memory_space=pltpu.HBM)
+    hbm, vmem = pl.BlockSpec(memory_space=pltpu.HBM), pl.BlockSpec(memory_space=pltpu.VMEM)
+    keep = functools.partial(pltpu.with_memory_space_constraint, memory_space=pltpu.HBM)
+    near = functools.partial(pltpu.with_memory_space_constraint, memory_space=pltpu.VMEM)
     f32, bf16, i32 = jnp.float32, jnp.bfloat16, jnp.int32
     extended = (nb, rows + 2 * EDGE, LANES)
     r_table = (kr, rows + GROUP, LANES)
@@ -335,19 +335,17 @@
     return pl.pallas_call(
         functools.partial(kernel, dims),
         name="redatum",
-        out_shape=jax.ShapeDtypeStruct((peers, 1, per_peer, nt), bf16),
-        in_specs=[hbm] * 8,
+        out_shape=pltpu.VMEM((peers, 1, per_peer, nt), bf16),
+        in_specs=[hbm] * 4 + [vmem] * 2 + [hbm] * 2,
         out_specs=pl.BlockSpec(memory_space=pltpu.VMEM),
         scratch_shapes=[
             pltpu.SMEM((1,), i32),
             pltpu.SMEM((kr,), f32),
             pltpu.SMEM((ks,), f32),
             pltpu.VMEM((rows, nt), bf16),
-            pltpu.VMEM(rcv_delay.shape, i32),
-            pltpu.VMEM(rcv_delay.shape, i32),
             pltpu.VMEM(src_delay.shape, i32),
             pltpu.VMEM(src_delay.shape, i32),
-            pltpu.SemaphoreType.DMA((8,)),
+            pltpu.SemaphoreType.DMA((6,)),
             pltpu.VMEM((LANES, LANES), i32),
             pltpu.VMEM((rows // LANES, LANES, LANES), i32),
             pltpu.VMEM(extended, f32),
@@ -371,9 +369,11 @@
             pltpu.SemaphoreType.DMA((peers,)),
         ],
         compiler_params=pltpu.CompilerParams(
-            collective_id=0, has_side_effects=True, vmem_limit_bytes=67_043_328
+            collective_id=0, has_side_effects=True, vmem_limit_bytes=60 * 2**20
         ),
-    )(live_count, rcv_taper, src_taper, traces, rcv_delay, rcv_frac, src_delay, src_frac)
+    )(
+        live_count, keep(rcv_taper), keep(src_taper), keep(traces), near(rcv_delay), near(rcv_frac), keep(src_delay), keep(src_frac)
+    )
 
 
 def solution(mesh):

time: 23 us -> 21.3 us (0.926)
  local copies, waits for them, and re-layouts: 1.77 us -> 0.77 us
  Pallas kernels: 20.4 us -> 19.6 us
    unnamed x1 -> x5, local copies, waits for them, and re-layouts: 1.77 us -> 0.77 us
    pallas_call x1, Pallas kernels: 20.4 us -> 19.6 us  [body(): pl.pallas_call(functools.partial(kernel, dims), name='redatum', out_shape...]
where the time goes in v1:
time: 21.3 us; the launch traced here: 21.1 us
  Pallas kernels  19.6 us (92%)
  local copies, waits for them, and re-layouts  0.77 us (4%)
  between operations  0.69 us (3%)
    pallas_call x1, Pallas kernels, body(): pl.pallas_call(functools.partial(kernel, dims), name='redatum', out_shape...  19.6 us
    unnamed x5, local copies, waits for them, and re-layouts  0.77 us

profile of v1, /device:TPU:0, one launch (start us, length us, event | category | flops | bytes accessed | tf_op | source)
XLA Modules:
  0.0 21.1 jit_solution(2830380911193056135)
XLA Ops:
  0.0 0.0 copy-start.1
  0.0 0.0 copy-start
  0.7 0.0 copy-done.1
  0.7 0.0 copy-done
  0.7 19.6 %redatum.1 = bf16[8,1,16,1536]{3,2,1,0:T(8,128)(2,1)S(1)} custom-call(s32[1]{0:T(128)S(6)} %copy.11.live_hbm, f32[9]{0:T(128)} %rtaper_hbm.1, f32[9]{0:T(128)} %staper_hbm.1, bf16[1,128,1536]{2,1,0:T(8,128)(2,1)} %x_hbm.1, s32[9,1,128]{2,1,0:T(1,128)S(1)} %bitcast.4, s32[9,1,128]{2,1,0:T(1,128)S(1)} %bitcast.5, s32[8,9,1,16]{3,2,1,0:T(1,128)} %bitcast.6, ...), custom_call_target="tpu_custom_call" | custom-call | tf_op jit(solution)/shard_map/redatum/pallas_call | solution.py:335
  20.3 0.7 %copy.10 = bf16[8,1,16,1536]{3,2,1,0:T(8,128)(2,1)} copy(bf16[8,1,16,1536]{3,2,1,0:T(8,128)(2,1)S(1)} %redatum.1) | data formatting | bytes 786432
Async XLA Ops:
  0.0 0.7 %copy-start.1 = (s32[1,128,9]{1,0,2:T(1,128)S(1)}, s32[1,128,9]{1,0,2:T(1,128)}, u32[]{:S(2)}) copy-start(s32[1,128,9]{1,0,2:T(1,128)} %param.10) | copy-start | bytes 13828
  0.0 0.7 %copy-start = (s32[1,128,9]{1,0,2:T(1,128)S(1)}, s32[1,128,9]{1,0,2:T(1,128)}, u32[]{:S(2)}) copy-start(s32[1,128,9]{1,0,2:T(1,128)} %param.9) | copy-start | bytes 13828

commit v2 on v1

--- a/solution.py
+++ b/solution.py
@@ -14,6 +14,8 @@
 LANES = 128
 GROUP = 8
 EDGE = 16
+FULL = 32000.0
+TINY = 1e-30
 MESH = pl.DeviceIdType.MESH
 
 
@@ -50,12 +52,19 @@
     return [jnp.where(is_last, rolled[b + 1], rolled[b]) for b in range(len(values))]
 
 
-def gathered(idx, own, mixed, nb):
-    now = mixed(0)
-    for b in range(nb):
-        after = mixed(b + 1) if b + 1 < nb else jnp.zeros_like(now)
-        yield b, jnp.take_along_axis(jnp.where(own, now, after), idx, axis=1)
-        now = after
+def words(values):
+    pairs = len(values) // 2
+    top = functools.reduce(jnp.maximum, [jnp.abs(v) for v in values])
+    top = jnp.maximum(jnp.max(top, axis=1, keepdims=True), TINY)
+    top = jnp.broadcast_to(top, values[0].shape)
+    scale = FULL / top
+    whole = [(v * scale).astype(jnp.int32) for v in values]
+    packed = [(whole[b] << 16) + whole[b + pairs] for b in range(pairs)]
+    return packed + [whole[pairs] << 16], top * (1.0 / (FULL * 65536.0))
+
+
+def unpacked(word):
+    return word.astype(jnp.float32), (word << 16).astype(jnp.float32)
 
 
 def kernel(
@@ -63,24 +72,24 @@
     live_hbm, rtaper_hbm, staper_hbm, x_hbm, rd_ref, rf_ref, sd_hbm, sf_hbm,
     out_ref,
     live_ref, rtaper_ref, staper_ref, x_ref, sd_ref, sf_ref, in_sem,
-    flat, turned, near, near1, far, far1, halo, sec, got, acc,
+    flat, turned, near, near_unit, far, far_unit, halo, sec, got, sum0, sum1, sum2, sum3, acc0, acc1,
     r_d, r_c0, r_c1, r_norm, t_d, t_c0, t_c1,
     halo_send, halo_recv, send_sem, recv_sem,
 ):
     rows, nt, peers, per_peer, n_rcv, kr, ks = dims
     nb = nt // LANES
+    pairs = nb // 2
     chunks = pl.cdiv(per_peer, GROUP)
-    used = min(GROUP, per_peer)
     me = lax.axis_index("shot")
     side = lax.axis_index("rcv")
     other = 1 - side
     f32 = jnp.float32
 
-    pairs = (
+    copies = (
         (x_hbm.at[0], x_ref), (live_hbm, live_ref), (rtaper_hbm, rtaper_ref),
         (staper_hbm, staper_ref), (sd_hbm, sd_ref), (sf_hbm, sf_ref),
     )
-    loads = [pltpu.make_async_copy(a, b, in_sem.at[n]) for n, (a, b) in enumerate(pairs)]
+    loads = [pltpu.make_async_copy(a, b, in_sem.at[n]) for n, (a, b) in enumerate(copies)]
     for load in loads:
         load.start()
 
@@ -94,10 +103,10 @@
     pl.semaphore_signal(barrier, inc=1, device_id={"rcv": other}, device_id_type=MESH)
     lax.fori_loop(1, peers, greet, 0)
 
-    for b in range(nb):
-        for start in (0, EDGE + rows):
-            near[b, start : start + EDGE, :] = jnp.zeros((EDGE, LANES), f32)
-            near1[b, start : start + EDGE, :] = jnp.zeros((EDGE, LANES), f32)
+    for start in (0, EDGE + rows):
+        for b in range(pairs + 1):
+            near[b, start : start + EDGE, :] = jnp.zeros((EDGE, LANES), jnp.int32)
+        near_unit[start : start + EDGE, :] = jnp.zeros((EDGE, LANES), f32)
     flat[...] = jnp.zeros_like(flat)
 
     lane = lax.broadcasted_iota(jnp.int32, (GROUP, LANES), 1)
@@ -134,9 +143,7 @@
         r_norm[at, :] = 1.0 / jnp.sqrt(jnp.maximum(fold, 1.0))
         return carry
 
-    lax.fori_loop(0, rows // GROUP, receiver_tables, 0)
-
-    pl.semaphore_wait(barrier, peers)
+    lax.fori_loop(0, rows // GROUP, receiver_tables, 0, unroll=4)
 
     halo_copy = pltpu.make_async_remote_copy(
         src_ref=x_hbm.at[0, pl.ds(pl.multiple_of(other * (rows - EDGE), EDGE), EDGE), :],
@@ -146,13 +153,13 @@
         device_id={"rcv": other},
         device_id_type=MESH,
     )
-    halo_copy.start()
 
     def filter_rows(load, base):
         done = [v.astype(f32) for v in smooth([load(b).astype(f32) for b in range(nb)])]
-        for b, (value, value1) in enumerate(zip(done, ahead(done))):
-            near[b, pl.ds(base, EDGE), :] = value
-            near1[b, pl.ds(base, EDGE), :] = value1
+        packed, unit = words(done)
+        for b, word in enumerate(packed):
+            near[b, pl.ds(base, EDGE), :] = word
+        near_unit[pl.ds(base, EDGE), :] = unit
 
     def filter_own(g, carry):
         start = pl.multiple_of(g * EDGE, EDGE)
@@ -160,13 +167,28 @@
         return carry
 
     loads[0].wait()
-    lax.fori_loop(0, rows // EDGE, filter_own, 0)
+    lax.fori_loop(0, rows // EDGE, filter_own, 0, unroll=4)
 
     edge_peer = other * (peers - 1)
 
-    def partner(i, sign):
-        step = peers // 2 + (1 - 2 * lax.rem(i, 2)) * ((i + 1) // 2)
-        return lax.rem(me + sign * step + 2 * peers, peers)
+    half = max(peers // 2, 1)
+    mine = me // half
+    place = lax.rem(me, half)
+
+    def source(i):
+        return half * lax.rem(mine + i // half, peers // half) + lax.rem(place + peers - i, half)
+
+    edge_here = jnp.where(edge_peer // half == mine, 1, 0)
+    across = half - 1 + edge_here
+
+    def target(i):
+        near_side = jnp.where(i < across, 0, 1)
+        step = i - near_side * across
+        span = jnp.where(near_side == edge_here, half - 1, half)
+        base = jnp.where(near_side == edge_here, side, 0)
+        local = base + lax.rem(place + step, jnp.maximum(span, 1))
+        block = lax.rem(mine + 1 + near_side, peers // half)
+        return jnp.where(i == peers - 1, edge_peer, half * block + local)
 
     def send_of(to):
         return pltpu.make_async_remote_copy(
@@ -188,44 +210,76 @@
             device_id_type=MESH,
         )
 
-    def receiver_step(i, carry):
-        to = partner(i, 1)
-
-        @pl.when(to == edge_peer)
-        def _():
-            halo_copy.wait_recv()
-            filter_rows(
-                lambda b: halo[:, b * LANES : (b + 1) * LANES],
-                pl.multiple_of(other * (EDGE + rows), EDGE),
-            )
-
+    def gather(to, sums):
         for c in range(chunks):
             row0 = to * per_peer + c * GROUP
             if per_peer % GROUP == 0:
                 row0 = pl.multiple_of(row0, GROUP)
             at = pl.ds(row0, GROUP)
-            total = [None] * nb
+            total0, total1 = [None] * nb, [None] * nb
             for a in range(kr):
-                d, c0, c1 = r_d[a, at, :], r_c0[a, at, :], r_c1[a, at, :]
+                d = r_d[a, at, :]
                 source = pl.ds(EDGE - AR + row0 + a, GROUP)
-
-                def mixed(b):
-                    return c0 * near[b, source, :] + c1 * near1[b, source, :]
-
-                for b, value in gathered((lane + d) & (LANES - 1), lane >= d, mixed, nb):
-                    total[b] = value if a == 0 else total[b] + value
+                unit = near_unit[source, :]
+                c0, c1 = r_c0[a, at, :] * unit, r_c1[a, at, :] * unit
+                idx, own = (lane + d) & (LANES - 1), lane >= d
+                now = near[0, source, :]
+                for b in range(pairs):
+                    after = near[b + 1, source, :]
+                    word = jnp.take_along_axis(jnp.where(own, now, after), idx, axis=1)
+                    now = after
+                    for n, value in zip((b, b + pairs), unpacked(word)):
+                        total0[n] = c0 * value if a == 0 else total0[n] + c0 * value
+                        total1[n] = c1 * value if a == 0 else total1[n] + c1 * value
             norm = r_norm[at, :]
-            one = [(v * norm).astype(jnp.bfloat16).astype(f32) for v in total]
-            for b, value in enumerate(smooth(one)):
-                sec[to, c * GROUP : c * GROUP + used, b * LANES : (b + 1) * LANES] = value[:used]
-
-        @pl.when(i < peers - 1)
+            rows_of = slice(c * GROUP, c * GROUP + GROUP)
+            for b in range(nb):
+                sums[0][b, rows_of, :] = total0[b] * norm
+                sums[1][b, rows_of, :] = total1[b] * norm
+
+    def emit(to, sums):
+        later = ahead([sums[1][b].astype(jnp.bfloat16).astype(f32) for b in range(nb)])
+        one = [(sums[0][b] + later[b]).astype(jnp.bfloat16).astype(f32) for b in range(nb)]
+        for b, value in enumerate(smooth(one)):
+            sec[to, :, b * LANES : (b + 1) * LANES] = value[:per_peer]
+
+
+    def dispatch(to):
+        @pl.when(to != me)
         def _():
             send_of(to).start()
 
-        return carry
-
-    lax.fori_loop(0, peers, receiver_step, 0)
+        @pl.when(to == me)
+        def _():
+            got[me] = sec[me]
+
+    even, odd = (sum0, sum1), (sum2, sum3)
+    gather(target(0), even)
+    emit(target(0), even)
+    pl.semaphore_wait(barrier, peers)
+    halo_copy.start()
+    dispatch(target(0))
+    if peers > 1:
+        gather(target(1), odd)
+
+        def receiver_steps(n, carry):
+            for i, now, then in ((2 * n + 1, odd, even), (2 * n + 2, even, odd)):
+                @pl.when(i == peers - 2)
+                def _():
+                    halo_copy.wait_recv()
+                    filter_rows(
+                        lambda b: halo[:, b * LANES : (b + 1) * LANES],
+                        pl.multiple_of(other * (EDGE + rows), EDGE),
+                    )
+
+                gather(target(i + 1), then)
+                emit(target(i), now)
+                dispatch(target(i))
+            return carry
+
+        lax.fori_loop(0, peers // 2 - 1, receiver_steps, 0)
+        emit(target(peers - 1), odd)
+        dispatch(target(peers - 1))
 
     for n in (3, 4, 5):
         loads[n].wait()
@@ -256,22 +310,23 @@
 
     def clear(k, carry):
         for b in range(nb):
-            acc[k, b] = jnp.zeros(acc.shape[2:], f32)
+            acc0[k, b] = jnp.zeros(acc0.shape[2:], f32)
+            acc1[k, b] = jnp.zeros(acc1.shape[2:], f32)
         return carry
 
     lax.fori_loop(0, peers, clear, 0)
 
     if per_peer < GROUP:
-        for b in range(nb):
-            far[b] = jnp.zeros(far.shape[1:], f32)
-            far1[b] = jnp.zeros(far.shape[1:], f32)
+        for b in range(pairs + 1):
+            far[b] = jnp.zeros(far.shape[1:], jnp.int32)
+        far_unit[...] = jnp.zeros(far_unit.shape, f32)
     width = min(peers, ks)
 
     def shot_sum(p, block_of):
-        done = [block_of(b).astype(f32) for b in range(nb)]
-        for b, (value, value1) in enumerate(zip(done, ahead(done))):
-            far[b, :per_peer, :] = value
-            far1[b, :per_peer, :] = value1
+        packed, unit = words([block_of(b).astype(f32) for b in range(nb)])
+        for b, word in enumerate(packed):
+            far[b, :per_peer, :] = word
+        far_unit[:per_peer, :] = unit
         base = 0 if width == peers else jnp.minimum(jnp.maximum(p - AS, 0), peers - width)
         for kk in range(width):
             k = base + kk
@@ -280,38 +335,46 @@
             inside = jnp.where(tap == a, 1.0, 0.0)
             for c in range(chunks):
                 at = slice(c * GROUP, c * GROUP + GROUP)
-                d, c0, c1 = t_d[k, a, at, :], t_c0[k, a, at, :] * inside, t_c1[k, a, at, :] * inside
-
-                def mixed(b):
-                    return c0 * far[b, at, :] + c1 * far1[b, at, :]
-
-                for b, value in gathered((lane + d) & (LANES - 1), lane >= d, mixed, nb):
-                    acc[k, b, at, :] += value
-
-    shot_sum(me, lambda b: sec[me, :, b * LANES : (b + 1) * LANES])
+                d, unit = t_d[k, a, at, :], far_unit[at, :] * inside
+                c0, c1 = t_c0[k, a, at, :] * unit, t_c1[k, a, at, :] * unit
+                idx, own = (lane + d) & (LANES - 1), lane >= d
+                now = far[0, at, :]
+                for b in range(pairs):
+                    after = far[b + 1, at, :]
+                    word = jnp.take_along_axis(jnp.where(own, now, after), idx, axis=1)
+                    now = after
+                    for n, value in zip((b, b + pairs), unpacked(word)):
+                        acc0[k, n, at, :] += c0 * value
+                        acc1[k, n, at, :] += c1 * value
 
     def source_step(i, carry):
-        origin = partner(i, -1)
-        recv_of(origin).wait_recv()
+        origin = source(i)
+
+        @pl.when(i > 0)
+        def _():
+            recv_of(origin).wait_recv()
+
         shot_sum(origin, lambda b: got[origin, :, b * LANES : (b + 1) * LANES])
         return carry
 
-    lax.fori_loop(0, peers - 1, source_step, 0)
+    lax.fori_loop(0, peers, source_step, 0)
 
     def finish(k, carry):
+        later = ahead([acc1[k, b].astype(jnp.bfloat16).astype(f32) for b in range(nb)])
         for b in range(nb):
-            out_ref[k, 0, :, b * LANES : (b + 1) * LANES] = acc[k, b, :per_peer, :].astype(jnp.bfloat16)
-        return carry
-
-    lax.fori_loop(0, peers, finish, 0)
+            value = (acc0[k, b] + later[b]).astype(jnp.bfloat16)
+            out_ref[k, 0, :, b * LANES : (b + 1) * LANES] = value[:per_peer]
+        return carry
+
+    lax.fori_loop(0, peers, finish, 0, unroll=4)
 
     halo_copy.wait_send()
 
     def drain(i, carry):
-        send_of(partner(i, 1)).wait_send()
-        return carry
-
-    lax.fori_loop(0, peers - 1, drain, 0)
+        send_of(source(i)).wait_send()
+        return carry
+
+    lax.fori_loop(1, peers, drain, 0)
 
 
 def body(traces, rcv_delay, rcv_frac, live_count, src_delay, src_frac, rcv_taper, src_taper):
@@ -329,7 +392,7 @@
     keep = functools.partial(pltpu.with_memory_space_constraint, memory_space=pltpu.HBM)
     near = functools.partial(pltpu.with_memory_space_constraint, memory_space=pltpu.VMEM)
     f32, bf16, i32 = jnp.float32, jnp.bfloat16, jnp.int32
-    extended = (nb, rows + 2 * EDGE, LANES)
+    extended = (nb // 2 + 1, rows + 2 * EDGE, LANES)
     r_table = (kr, rows + GROUP, LANES)
     t_table = (peers, ks, tall, LANES)
     return pl.pallas_call(
@@ -348,13 +411,18 @@
             pltpu.SemaphoreType.DMA((6,)),
             pltpu.VMEM((LANES, LANES), i32),
             pltpu.VMEM((rows // LANES, LANES, LANES), i32),
-            pltpu.VMEM(extended, f32),
-            pltpu.VMEM(extended, f32),
-            pltpu.VMEM((nb, tall, LANES), f32),
-            pltpu.VMEM((nb, tall, LANES), f32),
+            pltpu.VMEM(extended, i32),
+            pltpu.VMEM(extended[1:], f32),
+            pltpu.VMEM((nb // 2 + 1, tall, LANES), i32),
+            pltpu.VMEM((tall, LANES), f32),
             pltpu.VMEM((EDGE, nt), bf16),
             pltpu.VMEM((peers, per_peer, nt), bf16),
             pltpu.VMEM((peers, per_peer, nt), bf16),
+            pltpu.VMEM((nb, tall, LANES), f32),
+            pltpu.VMEM((nb, tall, LANES), f32),
+            pltpu.VMEM((nb, tall, LANES), f32),
+            pltpu.VMEM((nb, tall, LANES), f32),
+            pltpu.VMEM((peers, nb, tall, LANES), f32),
             pltpu.VMEM((peers, nb, tall, LANES), f32),
             pltpu.VMEM(r_table, i32),
             pltpu.VMEM(r_table, f32),

time: 21.3 us -> 19.7 us (0.925)
  Pallas kernels: 19.6 us -> 18 us
    pallas_call x1, Pallas kernels: 19.6 us -> 18 us  [body(): pl.pallas_call(functools.partial(kernel, dims), name='redatum', out_shape...]
where the time goes in v2:
time: 19.7 us; the launch traced here: 19.5 us
  Pallas kernels  18 us (91%)
  local copies, waits for them, and re-layouts  0.77 us (4%)
  between operations  0.69 us (4%)
    pallas_call x1, Pallas kernels, body(): pl.pallas_call(functools.partial(kernel, dims), name='redatum', out_shape...  18 us
    unnamed x5, local copies, waits for them, and re-layouts  0.77 us

profile of v2, /device:TPU:0, one launch (start us, length us, event | category | flops | bytes accessed | tf_op | source)
XLA Modules:
  0.0 19.5 jit_solution(13347090289405224800)
XLA Ops:
  0.0 0.0 copy-start.1
  0.0 0.0 copy-start
  0.7 0.0 copy-done.1
  0.7 0.0 copy-done
  0.7 18.0 %redatum.1 = bf16[8,1,16,1536]{3,2,1,0:T(8,128)(2,1)S(1)} custom-call(s32[1]{0:T(128)S(6)} %copy.11.live_hbm, f32[9]{0:T(128)} %rtaper_hbm.1, f32[9]{0:T(128)} %staper_hbm.1, bf16[1,128,1536]{2,1,0:T(8,128)(2,1)} %x_hbm.1, s32[9,1,128]{2,1,0:T(1,128)S(1)} %bitcast.4, s32[9,1,128]{2,1,0:T(1,128)S(1)} %bitcast.5, s32[8,9,1,16]{3,2,1,0:T(1,128)} %bitcast.6, ...), custom_call_target="tpu_custom_call" | custom-call | tf_op jit(solution)/shard_map/redatum/pallas_call | solution.py:398
  18.7 0.7 %copy.10 = bf16[8,1,16,1536]{3,2,1,0:T(8,128)(2,1)} copy(bf16[8,1,16,1536]{3,2,1,0:T(8,128)(2,1)S(1)} %redatum.1) | data formatting | bytes 786432
Async XLA Ops:
  0.0 0.7 %copy-start.1 = (s32[1,128,9]{1,0,2:T(1,128)S(1)}, s32[1,128,9]{1,0,2:T(1,128)}, u32[]{:S(2)}) copy-start(s32[1,128,9]{1,0,2:T(1,128)} %param.10) | copy-start | bytes 13828
  0.0 0.7 %copy-start = (s32[1,128,9]{1,0,2:T(1,128)S(1)}, s32[1,128,9]{1,0,2:T(1,128)}, u32[]{:S(2)}) copy-start(s32[1,128,9]{1,0,2:T(1,128)} %param.9) | copy-start | bytes 13828

commit v3 on v2

--- a/solution.py
+++ b/solution.py
@@ -72,8 +72,8 @@
     live_hbm, rtaper_hbm, staper_hbm, x_hbm, rd_ref, rf_ref, sd_hbm, sf_hbm,
     out_ref,
     live_ref, rtaper_ref, staper_ref, x_ref, sd_ref, sf_ref, in_sem,
-    flat, turned, near, near_unit, far, far_unit, halo, sec, got, sum0, sum1, sum2, sum3, acc0, acc1,
-    r_d, r_c0, r_c1, r_norm, t_d, t_c0, t_c1,
+    flat, turned, near, near_unit, far, far_unit, far1, far1_unit, halo, sec, got, sum0, sum1, sum2, sum3, acc0, acc1,
+    r_d, r_w, t_d, t_c0, t_c1,
     halo_send, halo_recv, send_sem, recv_sem,
 ):
     rows, nt, peers, per_peer, n_rcv, kr, ks = dims
@@ -100,7 +100,10 @@
         pl.semaphore_signal(barrier, inc=1, device_id={"shot": to}, device_id_type=MESH)
         return carry
 
-    pl.semaphore_signal(barrier, inc=1, device_id={"rcv": other}, device_id_type=MESH)
+    @pl.when(side == 0)
+    def _():
+        pl.semaphore_signal(barrier, inc=1, device_id={"rcv": other}, device_id_type=MESH)
+
     lax.fori_loop(1, peers, greet, 0)
 
     for start in (0, EDGE + rows):
@@ -116,9 +119,6 @@
         packed = jnp.broadcast_to(column, (GROUP, LANES))
         return packed >> 8, (packed & 255).astype(f32) * (1.0 / 256.0)
 
-    loads[1].wait()
-    loads[2].wait()
-    live_count = live_ref[0]
     for block in range(rows // LANES):
         cols = slice(block * LANES, (block + 1) * LANES)
         for a in range(kr):
@@ -128,19 +128,10 @@
     def receiver_tables(g, carry):
         at = pl.ds(pl.multiple_of(g * GROUP, GROUP), GROUP)
         columns = turned[g // (LANES // GROUP), pl.ds(pl.multiple_of(lax.rem(g, LANES // GROUP) * GROUP, GROUP), GROUP), :]
-        where0 = side * rows + g * GROUP + sub - AR
-        fold = jnp.zeros((GROUP, LANES), f32)
         for a in range(kr):
             d, weight = spread(columns[:, a : a + 1])
-            where = where0 + a
-            live = (where >= 0) & (where < rows * n_rcv) & (where < live_count)
-            live = live.astype(f32)
-            fold = fold + live
-            scale = rtaper_ref[a] * live
             r_d[a, at, :] = d
-            r_c0[a, at, :] = scale * (1.0 - weight)
-            r_c1[a, at, :] = scale * weight
-        r_norm[at, :] = 1.0 / jnp.sqrt(jnp.maximum(fold, 1.0))
+            r_w[a, at, :] = weight
         return carry
 
     lax.fori_loop(0, rows // GROUP, receiver_tables, 0, unroll=4)
@@ -157,6 +148,8 @@
     def filter_rows(load, base):
         done = [v.astype(f32) for v in smooth([load(b).astype(f32) for b in range(nb)])]
         packed, unit = words(done)
+        where = side * rows + base - EDGE + lax.broadcasted_iota(jnp.int32, (EDGE, LANES), 0)
+        unit = jnp.where(where < live_count, unit, 0.0)
         for b, word in enumerate(packed):
             near[b, pl.ds(base, EDGE), :] = word
         near_unit[pl.ds(base, EDGE), :] = unit
@@ -166,29 +159,43 @@
         filter_rows(lambda b: x_ref[pl.ds(start, EDGE), b * LANES : (b + 1) * LANES], EDGE + start)
         return carry
 
-    loads[0].wait()
-    lax.fori_loop(0, rows // EDGE, filter_own, 0, unroll=4)
+    for n in range(3):
+        loads[n].wait()
+    live_count = live_ref[0]
 
     edge_peer = other * (peers - 1)
 
     half = max(peers // 2, 1)
-    mine = me // half
-    place = lax.rem(me, half)
+
+    def across(m):
+        total, unit = 0, 1
+        while unit < peers:
+            x, y = lax.rem(me // unit, 2), lax.rem(m // unit, 2)
+            total = total + unit * (x + y - 2 * x * y)
+            unit *= 2
+        return total
+
+    def partner(m, i):
+        return across(m) if peers & (peers - 1) == 0 else lax.rem(me + i, peers)
 
     def source(i):
-        return half * lax.rem(mine + i // half, peers // half) + lax.rem(place + peers - i, half)
-
-    edge_here = jnp.where(edge_peer // half == mine, 1, 0)
-    across = half - 1 + edge_here
+        far_half = half + (i - half) + 1 - 2 * lax.rem(i, 2)
+        return partner(jnp.where(i == 0, 0, jnp.where(i < half, half - i, far_half)), i)
+
+    def rank(i):
+        return partner(jnp.where(i < half, half + i + 1 - 2 * lax.rem(i, 2), peers - 1 - i), i + 1)
+
+    def place_of(to):
+        if peers & (peers - 1):
+            return lax.rem(to - me - 1 + 2 * peers, peers)
+        m = across(to)
+        return jnp.where(m < half, peers - 1 - m, m - half + 1 - 2 * lax.rem(m, 2))
+
+    edge_place = place_of(edge_peer)
 
     def target(i):
-        near_side = jnp.where(i < across, 0, 1)
-        step = i - near_side * across
-        span = jnp.where(near_side == edge_here, half - 1, half)
-        base = jnp.where(near_side == edge_here, side, 0)
-        local = base + lax.rem(place + step, jnp.maximum(span, 1))
-        block = lax.rem(mine + 1 + near_side, peers // half)
-        return jnp.where(i == peers - 1, edge_peer, half * block + local)
+        skipped = jnp.where(i >= edge_place, i + 1, i)
+        return rank(jnp.where(i == peers - 1, edge_place, skipped))
 
     def send_of(to):
         return pltpu.make_async_remote_copy(
@@ -221,7 +228,9 @@
                 d = r_d[a, at, :]
                 source = pl.ds(EDGE - AR + row0 + a, GROUP)
                 unit = near_unit[source, :]
-                c0, c1 = r_c0[a, at, :] * unit, r_c1[a, at, :] * unit
+                whole = rtaper_ref[a] * unit
+                c1 = whole * r_w[a, at, :]
+                c0 = whole - c1
                 idx, own = (lane + d) & (LANES - 1), lane >= d
                 now = near[0, source, :]
                 for b in range(pairs):
@@ -231,7 +240,10 @@
                     for n, value in zip((b, b + pairs), unpacked(word)):
                         total0[n] = c0 * value if a == 0 else total0[n] + c0 * value
                         total1[n] = c1 * value if a == 0 else total1[n] + c1 * value
-            norm = r_norm[at, :]
+            where = side * rows + row0 + sub
+            last = jnp.minimum(jnp.minimum(live_count, rows * n_rcv) - 1, where + AR)
+            fold = last - jnp.maximum(where - AR, 0) + 1
+            norm = 1.0 / jnp.sqrt(jnp.maximum(fold, 1).astype(f32))
             rows_of = slice(c * GROUP, c * GROUP + GROUP)
             for b in range(nb):
                 sums[0][b, rows_of, :] = total0[b] * norm
@@ -254,11 +266,25 @@
             got[me] = sec[me]
 
     even, odd = (sum0, sum1), (sum2, sum3)
+    def filter_all():
+        lax.fori_loop(0, rows // EDGE, filter_own, 0, unroll=4)
+
+    if per_peer == EDGE:
+        for step in (-1, 0, 1):
+            filter_own(jnp.minimum(jnp.maximum(target(0) + step, 0), peers - 1), 0)
+    else:
+        filter_all()
     gather(target(0), even)
     emit(target(0), even)
-    pl.semaphore_wait(barrier, peers)
-    halo_copy.start()
+    pl.semaphore_wait(barrier, peers - 1 + side)
+
+    @pl.when(side == 1)
+    def _():
+        halo_copy.start()
+
     dispatch(target(0))
+    if per_peer == EDGE:
+        filter_all()
     if peers > 1:
         gather(target(1), odd)
 
@@ -267,6 +293,11 @@
                 @pl.when(i == peers - 2)
                 def _():
                     halo_copy.wait_recv()
+
+                    @pl.when(side == 0)
+                    def _():
+                        halo_copy.start()
+
                     filter_rows(
                         lambda b: halo[:, b * LANES : (b + 1) * LANES],
                         pl.multiple_of(other * (EDGE + rows), EDGE),
@@ -317,16 +348,18 @@
     lax.fori_loop(0, peers, clear, 0)
 
     if per_peer < GROUP:
-        for b in range(pairs + 1):
-            far[b] = jnp.zeros(far.shape[1:], jnp.int32)
-        far_unit[...] = jnp.zeros(far_unit.shape, f32)
+        for table in ((far, far_unit), (far1, far1_unit)):
+            table[0][...] = jnp.zeros(far.shape, jnp.int32)
+            table[1][...] = jnp.zeros(far_unit.shape, f32)
     width = min(peers, ks)
 
-    def shot_sum(p, block_of):
-        packed, unit = words([block_of(b).astype(f32) for b in range(nb)])
+    def prepare(p, table):
+        packed, unit = words([got[p, :, b * LANES : (b + 1) * LANES].astype(f32) for b in range(nb)])
         for b, word in enumerate(packed):
-            far[b, :per_peer, :] = word
-        far_unit[:per_peer, :] = unit
+            table[0][b, :per_peer, :] = word
+        table[1][:per_peer, :] = unit
+
+    def accumulate(p, table):
         base = 0 if width == peers else jnp.minimum(jnp.maximum(p - AS, 0), peers - width)
         for kk in range(width):
             k = base + kk
@@ -335,29 +368,39 @@
             inside = jnp.where(tap == a, 1.0, 0.0)
             for c in range(chunks):
                 at = slice(c * GROUP, c * GROUP + GROUP)
-                d, unit = t_d[k, a, at, :], far_unit[at, :] * inside
+                d, unit = t_d[k, a, at, :], table[1][at, :] * inside
                 c0, c1 = t_c0[k, a, at, :] * unit, t_c1[k, a, at, :] * unit
                 idx, own = (lane + d) & (LANES - 1), lane >= d
-                now = far[0, at, :]
+                now = table[0][0, at, :]
                 for b in range(pairs):
-                    after = far[b + 1, at, :]
+                    after = table[0][b + 1, at, :]
                     word = jnp.take_along_axis(jnp.where(own, now, after), idx, axis=1)
                     now = after
                     for n, value in zip((b, b + pairs), unpacked(word)):
                         acc0[k, n, at, :] += c0 * value
                         acc1[k, n, at, :] += c1 * value
 
-    def source_step(i, carry):
-        origin = source(i)
-
-        @pl.when(i > 0)
-        def _():
-            recv_of(origin).wait_recv()
-
-        shot_sum(origin, lambda b: got[origin, :, b * LANES : (b + 1) * LANES])
-        return carry
-
-    lax.fori_loop(0, peers, source_step, 0)
+    def arrive(i, table):
+        recv_of(source(i)).wait_recv()
+        prepare(source(i), table)
+
+    first, second = (far, far_unit), (far1, far1_unit)
+    prepare(me, first)
+
+    def source_steps(n, carry):
+        arrive(2 * n + 1, second)
+        accumulate(source(2 * n), first)
+        arrive(2 * n + 2, first)
+        accumulate(source(2 * n + 1), second)
+        return carry
+
+    if peers > 1:
+        lax.fori_loop(0, peers // 2 - 1, source_steps, 0)
+        arrive(peers - 1, second)
+        accumulate(source(peers - 2), first)
+        accumulate(source(peers - 1), second)
+    else:
+        accumulate(me, first)
 
     def finish(k, carry):
         later = ahead([acc1[k, b].astype(jnp.bfloat16).astype(f32) for b in range(nb)])
@@ -366,7 +409,7 @@
             out_ref[k, 0, :, b * LANES : (b + 1) * LANES] = value[:per_peer]
         return carry
 
-    lax.fori_loop(0, peers, finish, 0, unroll=4)
+    lax.fori_loop(0, peers, finish, 0, unroll=min(peers, 8))
 
     halo_copy.wait_send()
 
@@ -415,6 +458,8 @@
             pltpu.VMEM(extended[1:], f32),
             pltpu.VMEM((nb // 2 + 1, tall, LANES), i32),
             pltpu.VMEM((tall, LANES), f32),
+            pltpu.VMEM((nb // 2 + 1, tall, LANES), i32),
+            pltpu.VMEM((tall, LANES), f32),
             pltpu.VMEM((EDGE, nt), bf16),
             pltpu.VMEM((peers, per_peer, nt), bf16),
             pltpu.VMEM((peers, per_peer, nt), bf16),
@@ -426,8 +471,6 @@
             pltpu.VMEM((peers, nb, tall, LANES), f32),
             pltpu.VMEM(r_table, i32),
             pltpu.VMEM(r_table, f32),
-            pltpu.VMEM(r_table, f32),
-            pltpu.VMEM(r_table[1:], f32),
             pltpu.VMEM(t_table, i32),
             pltpu.VMEM(t_table, f32),
             pltpu.VMEM(t_table, f32),

time: 19.7 us -> 18.9 us (0.959)
  Pallas kernels: 18 us -> 17.2 us
    pallas_call x1, Pallas kernels: 18 us -> 17.2 us  [body(): pl.pallas_call(functools.partial(kernel, dims), name='redatum', out_shape...]
where the time goes in v3:
time: 18.9 us; the launch traced here: 18.6 us
  Pallas kernels  17.2 us (91%)
  local copies, waits for them, and re-layouts  0.77 us (4%)
  between operations  0.69 us (4%)
    pallas_call x1, Pallas kernels, body(): pl.pallas_call(functools.partial(kernel, dims), name='redatum', out_shape...  17.2 us
    unnamed x5, local copies, waits for them, and re-layouts  0.77 us

profile of v3, /device:TPU:0, one launch (start us, length us, event | category | flops | bytes accessed | tf_op | source)
XLA Modules:
  0.0 18.6 jit_solution(6488891087505064536)
XLA Ops:
  0.0 0.0 copy-start.1
  0.0 0.0 copy-start
  0.7 0.0 copy-done.1
  0.7 0.0 copy-done
  0.7 17.2 %redatum.1 = bf16[8,1,16,1536]{3,2,1,0:T(8,128)(2,1)S(1)} custom-call(s32[1]{0:T(128)S(6)} %copy.11.live_hbm, f32[9]{0:T(128)} %rtaper_hbm.1, f32[9]{0:T(128)} %staper_hbm.1, bf16[1,128,1536]{2,1,0:T(8,128)(2,1)} %x_hbm.1, s32[9,1,128]{2,1,0:T(1,128)S(1)} %bitcast.4, s32[9,1,128]{2,1,0:T(1,128)S(1)} %bitcast.5, s32[8,9,1,16]{3,2,1,0:T(1,128)} %bitcast.6, ...), custom_call_target="tpu_custom_call" | custom-call | tf_op jit(solution)/shard_map/redatum/pallas_call | solution.py:441
  17.9 0.7 %copy.10 = bf16[8,1,16,1536]{3,2,1,0:T(8,128)(2,1)} copy(bf16[8,1,16,1536]{3,2,1,0:T(8,128)(2,1)S(1)} %redatum.1) | data formatting | bytes 786432
Async XLA Ops:
  0.0 0.7 %copy-start.1 = (s32[1,128,9]{1,0,2:T(1,128)S(1)}, s32[1,128,9]{1,0,2:T(1,128)}, u32[]{:S(2)}) copy-start(s32[1,128,9]{1,0,2:T(1,128)} %param.10) | copy-start | bytes 13828
  0.0 0.7 %copy-start = (s32[1,128,9]{1,0,2:T(1,128)S(1)}, s32[1,128,9]{1,0,2:T(1,128)}, u32[]{:S(2)}) copy-start(s32[1,128,9]{1,0,2:T(1,128)} %param.9) | copy-start | bytes 13828

commit v4 on v3

--- a/solution.py
+++ b/solution.py
@@ -276,17 +276,29 @@
         filter_all()
     gather(target(0), even)
     emit(target(0), even)
-    pl.semaphore_wait(barrier, peers - 1 + side)
-
-    @pl.when(side == 1)
+    def enter():
+        pl.semaphore_wait(barrier, peers - 1 + side)
+
+        @pl.when(side == 1)
+        def _():
+            halo_copy.start()
+
+        dispatch(target(0))
+
+    @pl.when(me >= half)
     def _():
-        halo_copy.start()
-
-    dispatch(target(0))
+        enter()
+
     if per_peer == EDGE:
         filter_all()
     if peers > 1:
         gather(target(1), odd)
+
+    @pl.when(me < half)
+    def _():
+        enter()
+
+    if peers > 1:
 
         def receiver_steps(n, carry):
             for i, now, then in ((2 * n + 1, odd, even), (2 * n + 2, even, odd)):
@@ -330,6 +342,8 @@
                 at = slice(c * GROUP, c * GROUP + GROUP)
                 columns = turned[0, at, :]
                 for a in range(ks):
+                    if peers == group and not 0 <= kk + a - AS < peers:
+                        continue
                     d, weight = spread(columns[:, kk * EDGE + a : kk * EDGE + a + 1])
                     scale = staper_ref[a] * norm
                     t_d[k, a, at, :] = d

time: 18.9 us -> 18.9 us (level)
  the two profiles are of different devices: /device:TPU:0 before, /device:TPU:1 now
where the time goes in v4:
time: 18.9 us; the launch traced here: 18.7 us
  Pallas kernels  17.2 us (91%)
  local copies, waits for them, and re-layouts  0.77 us (4%)
  between operations  0.69 us (4%)
    pallas_call x1, Pallas kernels, body(): pl.pallas_call(functools.partial(kernel, dims), name='redatum', out_shape...  17.2 us
    unnamed x5, local copies, waits for them, and re-layouts  0.77 us

profile of v4, /device:TPU:1, one launch (start us, length us, event | category | flops | bytes accessed | tf_op | source)
XLA Modules:
  0.0 18.7 jit_solution(7212918881041237491)
XLA Ops:
  0.0 0.0 copy-start.1
  0.0 0.0 copy-start
  0.7 0.0 copy-done.1
  0.7 0.0 copy-done
  0.7 17.2 %redatum.1 = bf16[8,1,16,1536]{3,2,1,0:T(8,128)(2,1)S(1)} custom-call(s32[1]{0:T(128)S(6)} %copy.11.live_hbm, f32[9]{0:T(128)} %rtaper_hbm.1, f32[9]{0:T(128)} %staper_hbm.1, bf16[1,128,1536]{2,1,0:T(8,128)(2,1)} %x_hbm.1, s32[9,1,128]{2,1,0:T(1,128)S(1)} %bitcast.4, s32[9,1,128]{2,1,0:T(1,128)S(1)} %bitcast.5, s32[8,9,1,16]{3,2,1,0:T(1,128)} %bitcast.6, ...), custom_call_target="tpu_custom_call" | custom-call | tf_op jit(solution)/shard_map/redatum/pallas_call | solution.py:455
  18.0 0.7 %copy.10 = bf16[8,1,16,1536]{3,2,1,0:T(8,128)(2,1)} copy(bf16[8,1,16,1536]{3,2,1,0:T(8,128)(2,1)S(1)} %redatum.1) | data formatting | bytes 786432
Async XLA Ops:
  0.0 0.7 %copy-start.1 = (s32[1,128,9]{1,0,2:T(1,128)S(1)}, s32[1,128,9]{1,0,2:T(1,128)}, u32[]{:S(2)}) copy-start(s32[1,128,9]{1,0,2:T(1,128)} %param.10) | copy-start | bytes 13828
  0.0 0.7 %copy-start = (s32[1,128,9]{1,0,2:T(1,128)S(1)}, s32[1,128,9]{1,0,2:T(1,128)}, u32[]{:S(2)}) copy-start(s32[1,128,9]{1,0,2:T(1,128)} %param.9) | copy-start | bytes 13828

commit v5 on v4

--- a/solution.py
+++ b/solution.py
@@ -72,7 +72,7 @@
     live_hbm, rtaper_hbm, staper_hbm, x_hbm, rd_ref, rf_ref, sd_hbm, sf_hbm,
     out_ref,
     live_ref, rtaper_ref, staper_ref, x_ref, sd_ref, sf_ref, in_sem,
-    flat, turned, near, near_unit, far, far_unit, far1, far1_unit, halo, sec, got, sum0, sum1, sum2, sum3, acc0, acc1,
+    flat, band, turned, near, near_unit, far, far_unit, far1, far1_unit, halo, sec, got, sum0, sum1, sum2, sum3, acc0, acc1,
     r_d, r_w, t_d, t_c0, t_c1,
     halo_send, halo_recv, send_sem, recv_sem,
 ):
@@ -111,6 +111,10 @@
             near[b, start : start + EDGE, :] = jnp.zeros((EDGE, LANES), jnp.int32)
         near_unit[start : start + EDGE, :] = jnp.zeros((EDGE, LANES), f32)
     flat[...] = jnp.zeros_like(flat)
+
+    gap = lax.broadcasted_iota(jnp.int32, band.shape, 0) - lax.broadcasted_iota(jnp.int32, band.shape, 1) - LANES
+    near_taps = jnp.where(jnp.abs(gap) == 1, SIDE_TAP, 0.0)
+    band[...] = jnp.where(gap == 0, MAIN_TAP, near_taps).astype(jnp.bfloat16)
 
     lane = lax.broadcasted_iota(jnp.int32, (GROUP, LANES), 1)
     sub = lax.broadcasted_iota(jnp.int32, (GROUP, LANES), 0)
@@ -252,7 +256,15 @@
     def emit(to, sums):
         later = ahead([sums[1][b].astype(jnp.bfloat16).astype(f32) for b in range(nb)])
         one = [(sums[0][b] + later[b]).astype(jnp.bfloat16).astype(f32) for b in range(nb)]
-        for b, value in enumerate(smooth(one)):
+        if per_peer % EDGE == 0:
+            blank = jnp.zeros(one[0].shape, jnp.bfloat16)
+            padded = [blank] + [v.astype(jnp.bfloat16) for v in one] + [blank]
+            wide = [jnp.concatenate(padded[b : b + 3], axis=1) for b in range(nb)]
+            flat_out = jnp.dot(jnp.concatenate(wide, axis=0), band[...], preferred_element_type=f32)
+            done = [flat_out[b * per_peer : (b + 1) * per_peer].astype(jnp.bfloat16) for b in range(nb)]
+        else:
+            done = smooth(one)
+        for b, value in enumerate(done):
             sec[to, :, b * LANES : (b + 1) * LANES] = value[:per_peer]
 
 
@@ -467,6 +479,7 @@
             pltpu.VMEM(src_delay.shape, i32),
             pltpu.SemaphoreType.DMA((6,)),
             pltpu.VMEM((LANES, LANES), i32),
+            pltpu.VMEM((3 * LANES, LANES), bf16),
             pltpu.VMEM((rows // LANES, LANES, LANES), i32),
             pltpu.VMEM(extended, i32),
             pltpu.VMEM(extended[1:], f32),

time: 18.9 us -> 19 us (level)
  Pallas kernels: 17.2 us -> 17.4 us
where the time goes in v5:
time: 19 us; the launch traced here: 18.8 us
  Pallas kernels  17.4 us (92%)
  local copies, waits for them, and re-layouts  0.77 us (4%)
  between operations  0.69 us (4%)
    pallas_call x1, Pallas kernels, body(): pl.pallas_call(functools.partial(kernel, dims), name='redatum', out_shape...  17.4 us
    unnamed x5, local copies, waits for them, and re-layouts  0.77 us

profile of v5, /device:TPU:1, one launch (start us, length us, event | category | flops | bytes accessed | tf_op | source)
XLA Modules:
  0.0 18.8 jit_solution(8986816388329908865)
XLA Ops:
  0.0 0.0 copy-start.1
  0.0 0.0 copy-start
  0.7 0.0 copy-done.1
  0.7 0.0 copy-done
  0.7 17.4 %redatum.1 = bf16[8,1,16,1536]{3,2,1,0:T(8,128)(2,1)S(1)} custom-call(s32[1]{0:T(128)S(6)} %copy.11.live_hbm, f32[9]{0:T(128)} %rtaper_hbm.1, f32[9]{0:T(128)} %staper_hbm.1, bf16[1,128,1536]{2,1,0:T(8,128)(2,1)} %x_hbm.1, s32[9,1,128]{2,1,0:T(1,128)S(1)} %bitcast.4, s32[9,1,128]{2,1,0:T(1,128)S(1)} %bitcast.5, s32[8,9,1,16]{3,2,1,0:T(1,128)} %bitcast.6, ...), custom_call_target="tpu_custom_call" | custom-call | tf_op jit(solution)/shard_map/redatum/pallas_call | solution.py:467
  18.1 0.7 %copy.10 = bf16[8,1,16,1536]{3,2,1,0:T(8,128)(2,1)} copy(bf16[8,1,16,1536]{3,2,1,0:T(8,128)(2,1)S(1)} %redatum.1) | data formatting | bytes 786432
Async XLA Ops:
  0.0 0.7 %copy-start.1 = (s32[1,128,9]{1,0,2:T(1,128)S(1)}, s32[1,128,9]{1,0,2:T(1,128)}, u32[]{:S(2)}) copy-start(s32[1,128,9]{1,0,2:T(1,128)} %param.10) | copy-start | bytes 13828
  0.0 0.7 %copy-start = (s32[1,128,9]{1,0,2:T(1,128)S(1)}, s32[1,128,9]{1,0,2:T(1,128)}, u32[]{:S(2)}) copy-start(s32[1,128,9]{1,0,2:T(1,128)} %param.9) | copy-start | bytes 13828
